TPU v7x, 256 devices: a whole 4x4x8 slice. The times are simulated.
256 devices in a mesh: row: 32 (over z, y_lo, core), col: 8 (over x, y_hi).
Axes of the slice: x: 4, y: 4 (y_hi: 2, y_lo: 2; y = y_hi * 2 + y_lo), z: 8, core: 2. Of those that a mesh axis runs over, the one named last changes fastest.
Arguments:
- activations: bfloat16 [1024, 16384], P('col', 'row'), may hold values from -6 to 6
- out_grad: bfloat16 [1024, 16384], P('col', 'row'), may hold values from -2 to 2
- gate_pre: bfloat16 [1024, 8192], P('row', 'col'), may hold values from -6 to 6
- up_pre: bfloat16 [1024, 8192], P('row', 'col'), may hold values from -6 to 6
- gate_weight: bfloat16 [16384, 8192], P('row', 'col'), may hold values from -0.046875 to 0.046875
- up_weight: bfloat16 [16384, 8192], P('row', 'col'), may hold values from -0.046875 to 0.046875
- down_weight: bfloat16 [8192, 16384], P('col', 'row'), may hold values from -0.0625 to 0.0625
Outputs:
- input_grad: bfloat16 [1024, 16384], P('col', 'row')
- gate_grad: bfloat16 [16384, 8192], P('row', 'col')
- up_grad: bfloat16 [16384, 8192], P('row', 'col')
- down_grad: bfloat16 [8192, 16384], P('col', 'row')
All inputs are finite; a program needn't handle non-finite values.
Results may differ from a plain program's by a relative error of at most 0.0051.
Values may be sent and summed in bfloat16 or wider, within the bound.
A program may use at most 64 MiB of HBM per device.

v0:
```python
import jax
import jax.numpy as jnp
from jax import lax
from jax.sharding import PartitionSpec as P


def contract_rows(left, right):
    return lax.dot_general(
        left, right, (((0,), (0,)), ((), ())), preferred_element_type=jnp.float32
    )


def contract_cols(left, right):
    return lax.dot_general(
        left, right, (((1,), (1,)), ((), ())), preferred_element_type=jnp.float32
    )


def derive(hidden_grad, gate_pre, up_pre):
    gate_val = gate_pre.astype(jnp.float32)
    up_val = up_pre.astype(jnp.float32)
    gate_sig = jax.nn.sigmoid(gate_val)
    swish_val = gate_val * gate_sig
    hidden = (swish_val * up_val).astype(jnp.bfloat16)
    gate_back = (hidden_grad * up_val * gate_sig * (1.0 + gate_val * (1.0 - gate_sig))).astype(
        jnp.bfloat16
    )
    up_back = (hidden_grad * swish_val).astype(jnp.bfloat16)
    return (hidden, gate_back, up_back)


def per_device(activations, out_grad, gate_pre, up_pre, gate_weight, up_weight, down_weight):
    acts_all, grad_all = (
        lax.all_gather(activations, "col", axis=0, tiled=True),
        lax.all_gather(out_grad, "col", axis=0, tiled=True),
    )
    grad_rows = grad_all
    hidden_grad = lax.psum_scatter(
        contract_cols(grad_rows, down_weight), "row", scatter_dimension=0, tiled=True
    )
    hidden, gate_back, up_back = derive(hidden_grad, gate_pre, up_pre)
    hid_piece = lax.all_gather(hidden, "row", axis=0, tiled=True)
    gate_piece = lax.all_gather(gate_back, "row", axis=0, tiled=True)
    up_piece = lax.all_gather(up_back, "row", axis=0, tiled=True)
    grad_rows = grad_all
    down_acc = contract_rows(hid_piece, grad_rows)
    gate_acc = contract_rows(acts_all, gate_piece)
    up_acc = contract_rows(acts_all, up_piece)
    input_rows = contract_cols(gate_piece, gate_weight) + contract_cols(up_piece, up_weight)
    input_acc = input_rows
    down_acc, gate_acc, up_acc, input_acc = (down_acc, gate_acc, up_acc, input_acc)
    input_grad = lax.psum_scatter(input_acc, "col", scatter_dimension=0, tiled=True)
    return (
        input_grad.astype(jnp.bfloat16),
        gate_acc.astype(jnp.bfloat16),
        up_acc.astype(jnp.bfloat16),
        down_acc.astype(jnp.bfloat16),
    )


def solution(mesh):
    placed = (
        P("col", "row"),
        P("col", "row"),
        P("row", "col"),
        P("row", "col"),
        P("row", "col"),
        P("row", "col"),
        P("col", "row"),
    )
    return jax.shard_map(
        per_device,
        mesh=mesh,
        in_specs=placed,
        out_specs=(P("col", "row"), P("row", "col"), P("row", "col"), P("col", "row")),
        check_vma=False,
    )
```

profile of v0, /device:TPU:32, one launch (start us, length us, event | category | flops | bytes accessed | tf_op | source)
XLA Modules:
  0.0 538.8 jit_solution(6172015009212809988)
XLA Ops:
  7.2 0.0 copy-start
  7.2 0.0 all-gather.6.cloned.1.call-start
  7.2 0.7 all-gather.6.cloned.1.call-update
  7.9 0.0 reduce-scatter.3.cloned.1.call-start
  8.0 57.5 %all-gather.6.cloned.1.call-done = bf16[1024,512]{1,0:T(8,128)(2,1)} async-done(((bf16[128,512]{1,0:T(8,128)(2,1)}), bf16[1024,512]{1,0:T(8,128)(2,1)}) %all-gather.6.cloned.1.call-update) | async-done | bytes 1048592 | tf_op jit(solution)/shard_map/all_gather | solution.py:35
  65.5 0.0 copy-done
  65.5 4.4 fusion.10
  69.9 0.0 copy-start.1
  69.9 0.0 copy-start.2
  70.0 0.0 copy-start.3
  70.0 0.0 reduce-scatter.3.cloned.1.call-update
  70.0 0.0 all-gather.8.cloned.1.call-start
  70.0 117.0 %reduce-scatter.3.cloned.1.call-done = f32[32,1024]{1,0:T(8,128)} async-done(((f32[1024,1024]{1,0:T(8,128)}), f32[32,1024]{1,0:T(8,128)}) %reduce-scatter.3.cloned.1.call-update) | async-done | bytes 131088 | tf_op jit(solution)/shard_map/reduce_scatter | solution.py:38
  187.1 0.0 copy-done.1
  187.1 0.0 copy-done.2
  187.1 1.6 multiply_convert_fusion
  188.7 0.0 all-gather.8.cloned.1.call-update
  188.7 0.0 all-gather.10.cloned.1.call-start
  188.8 0.5 all-gather.10.cloned.1.call-update
  189.3 0.0 all-gather.12.cloned.1.call-start
  189.4 0.5 all-gather.12.cloned.1.call-update
  189.9 0.0 all-gather.14.cloned.1.call-start
  189.9 0.5 all-gather.14.cloned.1.call-update
  190.5 0.0 copy-start.4
  190.5 0.0 reduce-scatter.5.cloned.1.call-start
  190.5 67.7 %all-gather.8.cloned.1.call-done = bf16[1024,1024]{1,0:T(8,128)(2,1)} async-done(((bf16[32,1024]{1,0:T(8,128)(2,1)}), bf16[1024,1024]{1,0:T(8,128)(2,1)}) %all-gather.8.cloned.1.call-update) | async-done | bytes 2097168 | tf_op jit(solution)/shard_map/all_gather | solution.py:43
  258.2 0.0 copy-done.3
  258.2 4.2 fusion.11
  262.5 62.1 %all-gather.10.cloned.1.call-done = bf16[1024,1024]{1,0:T(8,128)(2,1)} async-done(((bf16[32,1024]{1,0:T(8,128)(2,1)}), bf16[1024,1024]{1,0:T(8,128)(2,1)}) %all-gather.10.cloned.1.call-update) | async-done | bytes 2097168 | tf_op jit(solution)/shard_map/all_gather | solution.py:44
  324.5 0.0 copy-done.4
  324.5 4.9 convolution_add_fusion
  329.4 0.0 reduce-scatter.5.cloned.1.call-update
  329.5 50.4 %all-gather.12.cloned.1.call-done = bf16[1024,512]{1,0:T(8,128)(2,1)} async-done(((bf16[128,512]{1,0:T(8,128)(2,1)}), bf16[1024,512]{1,0:T(8,128)(2,1)}) %all-gather.12.cloned.1.call-update) | async-done | bytes 1048592 | tf_op jit(solution)/shard_map/all_gather | solution.py:34
  379.9 3.1 fusion
  383.0 0.0 copy-start.6
  383.0 1.3 copy.11
  384.3 0.0 copy-done.6
  384.3 2.9 fusion.1
  387.2 0.0 copy-start.5
  387.2 1.3 copy.12
  388.6 55.5 %all-gather.14.cloned.1.call-done = bf16[1024,1024]{1,0:T(8,128)(2,1)} async-done(((bf16[32,1024]{1,0:T(8,128)(2,1)}), bf16[1024,1024]{1,0:T(8,128)(2,1)}) %all-gather.14.cloned.1.call-update) | async-done | bytes 2097168 | tf_op jit(solution)/shard_map/all_gather | solution.py:42
  444.0 0.0 copy-done.5
  444.0 3.8 convolution_convert_fusion
  447.9 82.5 %reduce-scatter.5.cloned.1.call-done = f32[128,512]{1,0:T(8,128)} async-done(((f32[1024,512]{1,0:T(8,128)}), f32[128,512]{1,0:T(8,128)}) %reduce-scatter.5.cloned.1.call-update) | async-done | bytes 262160 | tf_op jit(solution)/shard_map/reduce_scatter | solution.py:52
  530.4 1.6 convert_element_type.37
Async XLA Ops:
  7.2 58.3 %copy-start = (bf16[1024,512]{1,0:T(8,128)(2,1)S(1)}, bf16[1024,512]{1,0:T(8,128)(2,1)}, u32[]{:S(2)}) copy-start(bf16[1024,512]{1,0:T(8,128)(2,1)} %param.13) | copy-start | bytes 3145732
  7.2 58.3 %all-gather.6.cloned.1.call-start = ((), (), s32[]{:S(2)}) async-start(), calls=%async_computation.2 | async-start | bytes 1179648 | tf_op jit(solution)/shard_map/all_gather | solution.py:35
  7.9 179.1 %reduce-scatter.3.cloned.1.call-start = ((), (), s32[]{:S(2)}) async-start(), calls=%async_computation.3 | async-start | bytes 4325376 | tf_op jit(solution)/shard_map/reduce_scatter | solution.py:38
  69.9 117.1 %copy-start.1 = (bf16[32,1024]{1,0:T(8,128)(2,1)S(1)}, bf16[32,1024]{1,0:T(8,128)(2,1)}, u32[]{:S(2)}) copy-start(bf16[32,1024]{1,0:T(8,128)(2,1)} %param.9) | copy-start | bytes 196612
  69.9 117.1 %copy-start.2 = (bf16[32,1024]{1,0:T(8,128)(2,1)S(1)}, bf16[32,1024]{1,0:T(8,128)(2,1)}, u32[]{:S(2)}) copy-start(bf16[32,1024]{1,0:T(8,128)(2,1)} %param.10) | copy-start | bytes 196612
  70.0 188.3 %copy-start.3 = (bf16[512,1024]{1,0:T(8,128)(2,1)S(1)}, bf16[512,1024]{1,0:T(8,128)(2,1)}, u32[]{:S(2)}) copy-start(bf16[512,1024]{1,0:T(8,128)(2,1)} %param.11) | copy-start | bytes 3145732
  70.0 188.2 %all-gather.8.cloned.1.call-start = ((), (), s32[]{:S(2)}) async-start(), calls=%async_computation.4 | async-start | bytes 2162688 | tf_op jit(solution)/shard_map/all_gather | solution.py:43
  188.7 135.8 %all-gather.10.cloned.1.call-start = ((), (), s32[]{:S(2)}) async-start(), calls=%async_computation.5 | async-start | bytes 2162688 | tf_op jit(solution)/shard_map/all_gather | solution.py:44
  189.3 190.6 %all-gather.12.cloned.1.call-start = ((), (), s32[]{:S(2)}) async-start(), calls=%async_computation.7 | async-start | bytes 1179648 | tf_op jit(solution)/shard_map/all_gather | solution.py:34
  189.9 254.2 %all-gather.14.cloned.1.call-start = ((), (), s32[]{:S(2)}) async-start(), calls=%async_computation.8 | async-start | bytes 2162688 | tf_op jit(solution)/shard_map/all_gather | solution.py:42
  190.5 134.1 %copy-start.4 = (bf16[512,1024]{1,0:T(8,128)(2,1)S(1)}, bf16[512,1024]{1,0:T(8,128)(2,1)}, u32[]{:S(2)}) copy-start(bf16[512,1024]{1,0:T(8,128)(2,1)} %param.12) | copy-start | bytes 3145732
  190.5 339.9 %reduce-scatter.5.cloned.1.call-start = ((), (), s32[]{:S(2)}) async-start(), calls=%async_computation.6 | async-start | bytes 2359296 | tf_op jit(solution)/shard_map/reduce_scatter | solution.py:52
  383.0 1.3 copy-start.6
  387.2 56.8 %copy-start.5 = (bf16[1024,512]{1,0:T(8,128)(2,1)S(1)}, bf16[1024,512]{1,0:T(8,128)(2,1)}, u32[]{:S(2)}) copy-start(bf16[1024,512]{1,0:T(8,128)(2,1)} %all-gather.6.cloned.1.call-done) | copy-start | bytes 3145732
Sparse Core Ops, SparseCore 0:
  10.6 54.8 all-gather.5
  70.1 116.9 reduce-scatter.2
  189.5 68.6 all-gather.7
  260.5 63.9 all-gather.9
  327.0 52.8 all-gather.11
  381.6 62.4 all-gather.13
  448.1 82.2 reduce-scatter.4
where the time goes:
time: 539 us
  waiting for transfers between devices  495 us (92%)
  matrix products  23.4 us (4%)
  between operations  14.2 us (3%)
    reduce_scatter x1, waiting for transfers between devices, per_device(): lax.psum_scatter(contract_cols(grad_rows, down_weight), 'row', scatter_di...  117 us
    reduce_scatter x1, waiting for transfers between devices, per_device(): lax.psum_scatter(input_acc, 'col', scatter_dimension=0, tiled=True)  82.5 us
    all_gather x1, waiting for transfers between devices, per_device(): gate_piece = lax.all_gather(gate_back, 'row', axis=0, tiled=True)  67.7 us
    all_gather x1, waiting for transfers between devices, per_device(): up_piece = lax.all_gather(up_back, 'row', axis=0, tiled=True)  62.1 us
    all_gather x1, waiting for transfers between devices, per_device(): lax.all_gather(out_grad, 'col', axis=0, tiled=True)  57.5 us
    all_gather x1, waiting for transfers between devices, per_device(): hid_piece = lax.all_gather(hidden, 'row', axis=0, tiled=True)  55.5 us
    all_gather x1, waiting for transfers between devices, per_device(): lax.all_gather(activations, 'col', axis=0, tiled=True)  50.4 us
    dot_general x3, matrix products, contract_cols(): lax.dot_general(left, right, (((1,), (1,)), ((), ())), preferred_element_...  13.6 us
  transfers between devices with their start and end apart: 7, of which 7 were waited for; matrix products, arithmetic and copies ran while one was open for 4% of the time, Pallas kernels for 0%

commit v1 on v0

--- a/solution.py
+++ b/solution.py
@@ -41,7 +41,10 @@
     hidden, gate_back, up_back = derive(hidden_grad, gate_pre, up_pre)
     hid_piece = lax.all_gather(hidden, "row", axis=0, tiled=True)
     gate_piece = lax.all_gather(gate_back, "row", axis=0, tiled=True)
-    up_piece = lax.all_gather(up_back, "row", axis=0, tiled=True)
+    up_piece = jnp.concatenate(
+        lax.all_to_all(jnp.stack([up_back for _ in range(lax.axis_size("row"))]), "row", 0, 0),
+        axis=0,
+    )
     grad_rows = grad_all
     down_acc = contract_rows(hid_piece, grad_rows)
     gate_acc = contract_rows(acts_all, gate_piece)

time: 539 us -> 488 us (0.905)
  waiting for transfers between devices: 495 us -> 428 us
  starting transfers between devices: 0.27 us -> 12.3 us
    all_gather x1 -> x0, waiting for transfers between devices: 62.1 us -> none  [per_device(): up_piece = lax.all_gather(up_back, 'row', axis=0, tiled=True)]
    all_to_all x0 -> x1, starting transfers between devices: none -> 12.1 us  [per_device(): lax.all_to_all(jnp.stack([up_back for _ in range(lax.axis_size('row'))]),...]
  transfers between devices with their start and end apart: 7 -> 7, of which waited for: 7 -> 6; matrix products, arithmetic and copies ran while one was open for 4% -> 5% of each run, Pallas kernels for 0% -> 0%
where the time goes in v1:
time: 488 us; the launch traced here: 487 us
  waiting for transfers between devices  428 us (88%)
  matrix products  23.7 us (5%)
  between operations  14.2 us (3%)
  starting transfers between devices  12.3 us (3%)
  local copies, waits for them, and re-layouts  5.31 us (1%)
    reduce_scatter x1, waiting for transfers between devices, per_device(): lax.psum_scatter(contract_cols(grad_rows, down_weight), 'row', scatter_di...  117 us
    reduce_scatter x1, waiting for transfers between devices, per_device(): lax.psum_scatter(input_acc, 'col', scatter_dimension=0, tiled=True)  82.3 us
    all_gather x1, waiting for transfers between devices, per_device(): gate_piece = lax.all_gather(gate_back, 'row', axis=0, tiled=True)  68.5 us
    all_gather x1, waiting for transfers between devices, per_device(): lax.all_gather(out_grad, 'col', axis=0, tiled=True)  57.5 us
    all_gather x1, waiting for transfers between devices, per_device(): hid_piece = lax.all_gather(hidden, 'row', axis=0, tiled=True)  54.1 us
    all_gather x1, waiting for transfers between devices, per_device(): lax.all_gather(activations, 'col', axis=0, tiled=True)  47.1 us
    dot_general x3, matrix products, contract_cols(): lax.dot_general(left, right, (((1,), (1,)), ((), ())), preferred_element_...  13.5 us
    all_to_all x1, starting transfers between devices, per_device(): lax.all_to_all(jnp.stack([up_back for _ in range(lax.axis_size('row'))]),...  12.1 us
  transfers between devices with their start and end apart: 7, of which 6 were waited for; matrix products, arithmetic and copies ran while one was open for 5% of the time, Pallas kernels for 0%

profile of v1, /device:TPU:32, one launch (start us, length us, event | category | flops | bytes accessed | tf_op | source)
XLA Modules:
  0.0 487.1 jit_solution(15038869222550834632)
XLA Ops:
  7.2 0.0 copy-start
  7.2 0.0 all-gather.5.cloned.1.call-start
  7.2 0.7 all-gather.5.cloned.1.call-update
  7.9 0.0 reduce-scatter.3.cloned.1.call-start
  8.0 57.5 %all-gather.5.cloned.1.call-done = bf16[1024,512]{1,0:T(8,128)(2,1)} async-done(((bf16[128,512]{1,0:T(8,128)(2,1)}), bf16[1024,512]{1,0:T(8,128)(2,1)}) %all-gather.5.cloned.1.call-update) | async-done | bytes 1048592 | tf_op jit(solution)/shard_map/all_gather | solution.py:35
  65.5 0.0 copy-done
  65.5 4.5 fusion.10
  70.0 0.0 copy-start.1
  70.0 0.0 copy-start.2
  70.0 0.0 reduce-scatter.3.cloned.1.call-update
  70.0 0.0 all-gather.7.cloned.1.call-start
  70.0 117.1 %reduce-scatter.3.cloned.1.call-done = f32[32,1024]{1,0:T(8,128)} async-done(((f32[1024,1024]{1,0:T(8,128)}), f32[32,1024]{1,0:T(8,128)}) %reduce-scatter.3.cloned.1.call-update) | async-done | bytes 131088 | tf_op jit(solution)/shard_map/reduce_scatter | solution.py:38
  187.1 0.0 copy-done.1
  187.1 0.0 copy-done.2
  187.1 1.6 multiply_convert_fusion
  188.7 0.0 all-gather.7.cloned.1.call-update
  188.8 0.0 all-gather.9.cloned.1.call-start
  188.8 0.5 all-gather.9.cloned.1.call-update
  189.4 1.6 stack.2
  191.0 12.1 %all-to-all-start = ((bf16[32,32,1024]{2,1,0:T(8,128)(2,1)}), bf16[32,32,1024]{2,1,0:T(8,128)(2,1)S(1)}, u32[]{:S(2)}, u32[]{:S(2)}) async-start(bf16[32,32,1024]{2,1,0:T(8,128)(2,1)} %stack.2), calls=%async_computation.1 | async-start | bytes 4194304 | tf_op jit(solution)/shard_map/all_to_all | solution.py:45
  203.1 0.0 all-gather.11.cloned.1.call-start
  203.1 0.5 all-gather.11.cloned.1.call-update
  203.7 0.0 reduce-scatter.5.cloned.1.call-start
  203.7 68.5 %all-gather.7.cloned.1.call-done = bf16[1024,1024]{1,0:T(8,128)(2,1)} async-done(((bf16[32,1024]{1,0:T(8,128)(2,1)}), bf16[1024,1024]{1,0:T(8,128)(2,1)}) %all-gather.7.cloned.1.call-update) | async-done | bytes 2097168 | tf_op jit(solution)/shard_map/all_gather | solution.py:43
  272.2 4.5 fusion.11
  276.7 0.0 all-to-all-done
  276.7 4.6 convolution_add_fusion
  281.2 0.0 reduce-scatter.5.cloned.1.call-update
  281.3 47.1 %all-gather.9.cloned.1.call-done = bf16[1024,512]{1,0:T(8,128)(2,1)} async-done(((bf16[128,512]{1,0:T(8,128)(2,1)}), bf16[1024,512]{1,0:T(8,128)(2,1)}) %all-gather.9.cloned.1.call-update) | async-done | bytes 1048592 | tf_op jit(solution)/shard_map/all_gather | solution.py:34
  328.3 3.5 fusion.1
  331.8 0.0 copy-start.4
  331.8 2.4 copy.12
  334.1 0.0 copy-done.4
  334.1 2.9 fusion
  337.0 0.0 copy-start.3
  337.0 1.3 copy.11
  338.3 54.1 %all-gather.11.cloned.1.call-done = bf16[1024,1024]{1,0:T(8,128)(2,1)} async-done(((bf16[32,1024]{1,0:T(8,128)(2,1)}), bf16[1024,1024]{1,0:T(8,128)(2,1)}) %all-gather.11.cloned.1.call-update) | async-done | bytes 2097168 | tf_op jit(solution)/shard_map/all_gather | solution.py:42
  392.5 0.0 copy-done.3
  392.5 3.8 convolution_convert_fusion
  396.3 82.3 %reduce-scatter.5.cloned.1.call-done = f32[128,512]{1,0:T(8,128)} async-done(((f32[1024,512]{1,0:T(8,128)}), f32[128,512]{1,0:T(8,128)}) %reduce-scatter.5.cloned.1.call-update) | async-done | bytes 262160 | tf_op jit(solution)/shard_map/reduce_scatter | solution.py:55
  478.6 1.6 convert_element_type.37
Async XLA Ops:
  7.2 58.3 %copy-start = (bf16[1024,512]{1,0:T(8,128)(2,1)S(1)}, bf16[1024,512]{1,0:T(8,128)(2,1)}, u32[]{:S(2)}) copy-start(bf16[1024,512]{1,0:T(8,128)(2,1)} %param.13) | copy-start | bytes 3145732
  7.2 58.3 %all-gather.5.cloned.1.call-start = ((), (), s32[]{:S(2)}) async-start(), calls=%async_computation.3 | async-start | bytes 1179648 | tf_op jit(solution)/shard_map/all_gather | solution.py:35
  7.9 179.2 %reduce-scatter.3.cloned.1.call-start = ((), (), s32[]{:S(2)}) async-start(), calls=%async_computation.4 | async-start | bytes 4325376 | tf_op jit(solution)/shard_map/reduce_scatter | solution.py:38
  70.0 117.1 %copy-start.1 = (bf16[32,1024]{1,0:T(8,128)(2,1)S(1)}, bf16[32,1024]{1,0:T(8,128)(2,1)}, u32[]{:S(2)}) copy-start(bf16[32,1024]{1,0:T(8,128)(2,1)} %param.9) | copy-start | bytes 196612
  70.0 117.1 %copy-start.2 = (bf16[32,1024]{1,0:T(8,128)(2,1)S(1)}, bf16[32,1024]{1,0:T(8,128)(2,1)}, u32[]{:S(2)}) copy-start(bf16[32,1024]{1,0:T(8,128)(2,1)} %param.10) | copy-start | bytes 196612
  70.0 202.2 %all-gather.7.cloned.1.call-start = ((), (), s32[]{:S(2)}) async-start(), calls=%async_computation.5 | async-start | bytes 2162688 | tf_op jit(solution)/shard_map/all_gather | solution.py:43
  188.8 139.5 %all-gather.9.cloned.1.call-start = ((), (), s32[]{:S(2)}) async-start(), calls=%async_computation.7 | async-start | bytes 1179648 | tf_op jit(solution)/shard_map/all_gather | solution.py:34
  191.0 85.7 %all-to-all-start = ((bf16[32,32,1024]{2,1,0:T(8,128)(2,1)}), bf16[32,32,1024]{2,1,0:T(8,128)(2,1)S(1)}, u32[]{:S(2)}, u32[]{:S(2)}) async-start(bf16[32,32,1024]{2,1,0:T(8,128)(2,1)} %stack.2), calls=%async_computation.1 | async-start | bytes 4194304 | tf_op jit(solution)/shard_map/all_to_all | solution.py:45
  203.1 189.4 %all-gather.11.cloned.1.call-start = ((), (), s32[]{:S(2)}) async-start(), calls=%async_computation.8 | async-start | bytes 2162688 | tf_op jit(solution)/shard_map/all_gather | solution.py:42
  203.7 275.0 %reduce-scatter.5.cloned.1.call-start = ((), (), s32[]{:S(2)}) async-start(), calls=%async_computation.6 | async-start | bytes 2359296 | tf_op jit(solution)/shard_map/reduce_scatter | solution.py:55
  331.8 2.4 copy-start.4
  337.0 55.5 %copy-start.3 = (bf16[1024,512]{1,0:T(8,128)(2,1)S(1)}, bf16[1024,512]{1,0:T(8,128)(2,1)}, u32[]{:S(2)}) copy-start(bf16[1024,512]{1,0:T(8,128)(2,1)} %all-gather.5.cloned.1.call-done) | copy-start | bytes 3145732
Sparse Core Ops, SparseCore 0:
  10.6 54.8 all-gather.4
  70.1 116.9 reduce-scatter.2
  189.5 82.5 all-gather.6
  274.7 53.6 all-gather.8
  330.0 62.4 all-gather.10
  396.4 82.2 reduce-scatter.4
